TPU v7x, 256 devices: a whole 4x4x8 slice. The times are simulated.
256 devices in a mesh: leaf: 32 (over z, y), head: 8 (over x, core).
Axes of the slice: x: 4, y: 4, z: 8, core: 2. Of those that a mesh axis runs over, the one named last changes fastest.
Arguments:
- query_in: bfloat16 [4096, 8192], P('leaf', 'head'), may hold values from -12 to 12
- key_in: bfloat16 [4096, 1024], P(('leaf', 'head')), may hold values from -12 to 12
- value_in: bfloat16 [4096, 1024], P(('leaf', 'head')), may hold values from -6 to 6
- out_grad: bfloat16 [4096, 8192], P('leaf', 'head'), may hold values from -6 to 6
- ancestry: int32 [32, 8], replicated, may hold values from -1 to 31, as said below
- node_len: int32 [32], replicated, may hold values from 64 to 128, as said below
Outputs:
- attended: bfloat16 [4096, 8192], P('leaf', 'head')
- query_grad: float32 [4096, 8192], P('leaf', 'head')
- key_grad: float32 [4096, 1024], P(('leaf', 'head'))
- value_grad: float32 [4096, 1024], P(('leaf', 'head'))
Inputs may be any that keep to these rules, and one draw needn't show every extreme that they name: `ancestry`: row g lists the ancestors of node g from the root, node 0, at column 0 down to node g itself at column depth(g), then -1; every ancestor of a node comes before it; nodes 0 to 3 form a chain. `node_len`: the root's length is 128, the last node's 128 // 2.
All inputs are finite; a program needn't handle non-finite values.
Results may differ from a plain program's by a relative error of at most 0.019.
Values may be sent and summed in bfloat16 or wider, within the bound.
No kernel may reach another device: no remote copies, remote signals or barrier semaphores. Data moves between devices by JAX's collectives and lax.ppermute only.
A program may use at most 64 MiB of HBM per device.

v0:
```python
import math

import jax
import jax.numpy as jnp
from jax import lax
from jax.sharding import PartitionSpec as P

QH = 64
KVH = 8
HD = 128
BLK = 128


start_level = -1e30
tile_rows = 256


def over_tiles(length, update, carry):
    tile_width = math.gcd(length, tile_rows)
    return lax.fori_loop(
        0,
        length // tile_width,
        lambda number, state: update(state, number * tile_width, tile_width),
        carry,
    )


def token_tags(length_table, first, amount):
    position = first + jnp.arange(amount, dtype=jnp.int32)
    lengths = lax.dynamic_slice_in_dim(length_table, first, amount, 0)
    return (jnp.where(position % BLK < lengths, position // BLK, -2), position)


def visible(ancestor_rows, query_position, key_tag, key_position):
    member = jnp.any(ancestor_rows[:, :, None] == key_tag[None, None, :], axis=1)
    own_node = query_position // BLK
    return member & (
        (key_tag[None, :] != own_node[:, None]) | (key_position[None, :] <= query_position[:, None])
    )


def logits_of(query_group, key_tile, allowed):
    key_count = key_tile.shape[0]
    key_rows = key_tile.reshape(key_count, query_group.shape[1], HD)
    raw = jnp.einsum(
        "tkgd,skd->kgts", query_group, key_rows, preferred_element_type=jnp.float32
    ) * HD ** (-0.5)
    return jnp.where(allowed[None, None], raw, -jnp.inf)


def forward_tile(state, query_group, key_tile, value_tile, allowed):
    row_top, total, accum = state
    logits = logits_of(query_group, key_tile, allowed)
    new_top = jnp.maximum(row_top, jnp.max(logits, axis=-1))
    factor = jnp.exp(row_top - new_top)
    expo = jnp.exp(logits - new_top[..., None])
    total = total * factor + jnp.sum(expo, axis=-1)
    value_rows = value_tile.reshape(value_tile.shape[0], query_group.shape[1], HD)
    accum = accum * factor[..., None] + jnp.einsum(
        "kgts,skd->kgtd", expo.astype(jnp.bfloat16), value_rows, preferred_element_type=jnp.float32
    )
    return (new_top, total, accum)


def gradient_tile(query_group, grad_group, lse, delta, key_tile, value_tile, allowed):
    logits = logits_of(query_group, key_tile, allowed)
    weights = jnp.exp(logits - lse[..., None])
    value_rows = value_tile.reshape(value_tile.shape[0], query_group.shape[1], HD)
    dprob = jnp.einsum("tkgd,skd->kgts", grad_group, value_rows, preferred_element_type=jnp.float32)
    dlogit = (weights * (dprob - delta[..., None])).astype(jnp.bfloat16)
    return (weights.astype(jnp.bfloat16), dlogit)


def per_device(query_in, key_in, value_in, out_grad, ancestry, node_len):
    key_local, value_local = (
        lax.all_to_all(key_in, "head", split_axis=1, concat_axis=0, tiled=True),
        lax.all_to_all(value_in, "head", split_axis=1, concat_axis=0, tiled=True),
    )
    rows = query_in.shape[0]
    key_heads = key_local.shape[1] // HD
    group = QH // KVH
    leaf_base = lax.axis_index("leaf") * rows
    length_table = jnp.repeat(node_len, BLK)
    ancestor_table = jnp.repeat(ancestry, BLK, axis=0)
    all_rows = length_table.shape[0]
    query_position = leaf_base + jnp.arange(rows, dtype=jnp.int32)
    query_ancestors = lax.dynamic_slice_in_dim(ancestor_table, leaf_base, rows, 0)
    query_group = query_in.reshape(rows, key_heads, group, HD)
    grad_group = out_grad.reshape(rows, key_heads, group, HD)
    initial = (
        jnp.full((key_heads, group, rows), start_level, jnp.float32),
        jnp.zeros((key_heads, group, rows), jnp.float32),
        jnp.zeros((key_heads, group, rows, HD), jnp.float32),
    )
    key_piece = lax.all_gather(key_local, "leaf", axis=0, tiled=True)
    value_piece = lax.all_gather(value_local, "leaf", axis=0, tiled=True)

    def update(inner, offset, tile_width):
        key_tile = lax.dynamic_slice_in_dim(key_piece, offset, tile_width, 0)
        value_tile = lax.dynamic_slice_in_dim(value_piece, offset, tile_width, 0)
        key_tag, key_position = token_tags(length_table, offset, tile_width)
        allowed = visible(query_ancestors, query_position, key_tag, key_position)
        return forward_tile(inner, query_group, key_tile, value_tile, allowed)

    row_top, total, accum = over_tiles(key_piece.shape[0], update, initial)
    key_all, value_all = (
        lax.all_gather(key_local, "leaf", axis=0, tiled=True),
        lax.all_gather(value_local, "leaf", axis=0, tiled=True),
    )
    output = (accum / total[..., None]).astype(jnp.bfloat16)
    log_total = row_top + jnp.log(total)
    delta = jnp.sum(
        grad_group.transpose(1, 2, 0, 3).astype(jnp.float32) * output.astype(jnp.float32), axis=-1
    )
    attended = output.transpose(2, 0, 1, 3).reshape(rows, key_heads * group * HD)
    query_zero = jnp.zeros((rows, key_heads, group, HD), jnp.float32)

    def update_both(state, offset, tile_width):
        query_acc, buffer = state
        key_tile = lax.dynamic_slice_in_dim(key_all, offset, tile_width, 0)
        value_tile = lax.dynamic_slice_in_dim(value_all, offset, tile_width, 0)
        key_tag, key_position = token_tags(length_table, offset, tile_width)
        allowed = visible(query_ancestors, query_position, key_tag, key_position)
        probs, dlogit = gradient_tile(
            query_group, grad_group, log_total, delta, key_tile, value_tile, allowed
        )
        key_rows = key_tile.reshape(tile_width, key_heads, HD)
        query_acc = query_acc + jnp.einsum(
            "kgts,skd->tkgd", dlogit, key_rows, preferred_element_type=jnp.float32
        )
        key_term = jnp.einsum(
            "kgts,tkgd->skd", dlogit, query_group, preferred_element_type=jnp.float32
        )
        value_term = jnp.einsum(
            "kgts,tkgd->skd", probs, grad_group, preferred_element_type=jnp.float32
        )
        both_terms = jnp.concatenate(
            [
                key_term.reshape(tile_width, key_heads * HD),
                value_term.reshape(tile_width, key_heads * HD),
            ],
            axis=1,
        )
        buffer = lax.dynamic_update_slice_in_dim(buffer, both_terms, offset, 0)
        return (query_acc, buffer)

    buffer_zero = jnp.zeros((all_rows, 2 * key_heads * HD), jnp.float32)
    query_sum, buffer = over_tiles(all_rows, update_both, (query_zero, buffer_zero))
    summed = lax.psum_scatter(
        buffer.astype(jnp.bfloat16), "leaf", scatter_dimension=0, tiled=True
    ).astype(jnp.float32)
    key_sum = summed[:, : key_heads * HD]
    value_grad = summed[:, key_heads * HD :]
    scale = HD ** (-0.5)
    query_grad = (query_sum * scale).reshape(rows, key_heads * group * HD)
    key_grad = key_sum * scale
    key_grad, value_grad = (
        lax.all_to_all(
            key_grad.astype(jnp.bfloat16), "head", split_axis=0, concat_axis=1, tiled=True
        ).astype(key_grad.dtype),
        lax.all_to_all(
            value_grad.astype(jnp.bfloat16), "head", split_axis=0, concat_axis=1, tiled=True
        ).astype(value_grad.dtype),
    )
    return (attended, query_grad, key_grad, value_grad)


def solution(mesh):
    return jax.shard_map(
        per_device,
        mesh=mesh,
        in_specs=(
            P("leaf", "head"),
            P(("leaf", "head"), None),
            P(("leaf", "head"), None),
            P("leaf", "head"),
            P(),
            P(),
        ),
        out_specs=(
            P("leaf", "head"),
            P("leaf", "head"),
            P(("leaf", "head"), None),
            P(("leaf", "head"), None),
        ),
        check_vma=False,
    )
```

profile of v0, /device:TPU:1, one launch (start us, length us, event | category | flops | bytes accessed | tf_op | source)
XLA Modules:
  0.0 555.6 jit_solution(12811123765744551282)
XLA Ops:
  7.9 11.0 %all_to_all.64 = bf16[16,8,128]{2,0,1:T(8,128)(2,1)} all-to-all(bf16[16,8,128]{2,0,1:T(8,128)(2,1)S(1)} %copy_bitcast_fusion.3), channel_id=1, replica_groups=mesh['leaf'=32,'head'=8] {'head'}, dimensions={1} | all-to-all | bytes 65536 | tf_op jit(solution)/shard_map/all_to_all | solution.py:76
  19.7 8.5 %all_to_all.65 = bf16[16,8,128]{2,0,1:T(8,128)(2,1)} all-to-all(bf16[16,8,128]{2,0,1:T(8,128)(2,1)S(1)} %copy_bitcast_fusion.2), channel_id=1, replica_groups=mesh['leaf'=32,'head'=8] {'head'}, dimensions={1} | all-to-all | bytes 65536 | tf_op jit(solution)/shard_map/all_to_all | solution.py:77
  31.8 59.2 %all-gather.3.cloned.1.call-done = bf16[4096,128]{1,0:T(8,128)(2,1)} async-done(((bf16[128,128]{1,0:T(8,128)(2,1)}), bf16[4096,128]{1,0:T(8,128)(2,1)}) %all-gather.3.cloned.1.call-update) | async-done | bytes 1048592 | tf_op jit(solution)/shard_map/all_gather | solution.py:95
  91.0 76.5 %all-gather.5.cloned.1.call-done = bf16[4096,128]{1,0:T(8,128)(2,1)} async-done(((bf16[128,128]{1,0:T(8,128)(2,1)}), bf16[4096,128]{1,0:T(8,128)(2,1)}) %all-gather.5.cloned.1.call-update) | async-done | bytes 1048592 | tf_op jit(solution)/shard_map/all_gather | solution.py:96
  167.5 56.2 %while.44 = (s32[]{:T(128)}, f32[1,8,128]{2,1,0:T(8,128)S(1)}, f32[1,8,128]{2,1,0:T(8,128)S(1)}, f32[1,8,128,128]{3,2,1,0:T(8,128)S(1)}, s32[128,8]{1,0:T(8,128)...) while((s32[]{:T(128)}, f32[1,8,128]{2,1,0:T(8,128)S(1)}, ...), condition=%wide.region_4.5_spmd.clone.clone.clone, body=%wide.region_0.4_spmd.clone.clone.clone.sunk | while | flops 137082496 | bytes 4862171 | solution.py:20
  169.6 1.4 fusion.87
  173.1 1.4 fusion.87
  176.6 1.4 fusion.87
  180.1 1.4 fusion.87
  183.6 1.4 fusion.87
  187.1 1.4 fusion.87
  190.7 1.4 fusion.87
  194.2 1.4 fusion.87
  197.7 1.4 fusion.87
  201.2 1.4 fusion.87
  204.7 1.4 fusion.87
  208.2 1.4 fusion.87
  211.7 1.4 fusion.87
  215.2 1.4 fusion.87
  218.8 1.4 fusion.87
  222.3 1.4 fusion.87
  224.8 81.0 %while.45 = (s32[]{:T(128)}, f32[128,1,8,128]{0,3,2,1:T(8,128)S(1)}, bf16[4096,256]{1,0:T(8,128)(2,1)S(1)}, bf16[4096,128]{1,0:T(8,128)(2,1)}, s32[128,8]{1,0:T(...) while((s32[]{:T(128)}, ...), condition=%wide.region_8.9_spmd.clone.clone.clone, body=%wide.region_6.8_spmd.clone.clone.clone.sunk | while | flops 338534016 | bytes 8147185 | solution.py:20
  225.6 1.2 fusion.99
  230.7 1.2 fusion.99
  233.6 1.2 fusion.101
  235.7 1.2 fusion.99
  240.8 1.2 fusion.99
  245.8 1.2 fusion.99
  248.8 1.2 fusion.101
  250.9 1.2 fusion.99
  256.0 1.2 fusion.99
  258.9 1.2 fusion.101
  261.0 1.2 fusion.99
  266.1 1.2 fusion.99
  271.1 1.2 fusion.99
  276.2 1.2 fusion.99
  281.3 1.2 fusion.99
  286.3 1.2 fusion.99
  291.4 1.2 fusion.99
  296.5 1.2 fusion.99
  301.5 1.2 fusion.99
  305.8 1.3 copy-done.1
  307.2 216.1 %reduce-scatter.2.cloned.1.call-done = bf16[128,256]{1,0:T(8,128)(2,1)} async-done(((bf16[4096,256]{1,0:T(8,128)(2,1)}), bf16[128,256]{1,0:T(8,128)(2,1)}) %reduce-scatter.2.cloned.1.call-update) | async-done | bytes 65552 | tf_op jit(solution)/shard_map/reduce_scatter | solution.py:149
  523.3 1.5 multiply_convert_fusion
  524.8 10.3 %all-to-all-start.2 = ((bf16[8,16,128]{2,1,0:T(8,128)(2,1)}), bf16[8,16,128]{2,1,0:T(8,128)(2,1)S(1)}, u32[]{:S(2)}, u32[]{:S(2)}) async-start(bf16[8,16,128]{2,1,0:T(8,128)(2,1)} %bitcast.14), calls=%async_computation.3 | async-start | bytes 65536 | tf_op jit(solution)/shard_map/all_to_all | solution.py:158
  537.6 2.2 all-to-all-done.2
  539.8 4.0 all-to-all-start.3
  544.4 4.1 all-to-all-done.3
  (387 shorter events, 99.7 us)
Async XLA Ops:
  7.2 0.8 copy-start
  7.2 24.5 %copy-start.4 = (s32[32]{0:T(128)S(1)}, s32[32]{0:T(128)}, u32[]{:S(2)}) copy-start(s32[32]{0:T(128)} %param.15) | copy-start | bytes 388
  7.2 83.8 %all-gather.3.cloned.1.call-start = ((), (), s32[]{:S(2)}) async-start(), calls=%async_computation.5 | async-start | bytes 1081344 | tf_op jit(solution)/shard_map/all_gather | solution.py:95
  18.9 148.6 %all-gather.5.cloned.1.call-start = ((), (), s32[]{:S(2)}) async-start(), calls=%async_computation.6 | async-start | bytes 1081344 | tf_op jit(solution)/shard_map/all_gather | solution.py:96
  28.2 495.1 %reduce-scatter.2.cloned.1.call-start = ((), (), s32[]{:S(2)}) async-start(), calls=%async_computation.7 | async-start | bytes 2162688 | tf_op jit(solution)/shard_map/reduce_scatter | solution.py:149
  305.8 1.3 copy-start.1
  305.8 229.3 %copy-start.2 = (bf16[1,8,128,128]{2,3,1,0:T(8,128)(2,1)S(1)}, bf16[1,8,128,128]{2,3,1,0:T(8,128)(2,1)}, u32[]{:S(2)}) copy-start(bf16[1,8,128,128]{2,3,1,0:T(8,128)(2,1)} %get-tuple-element.949) | copy-start | bytes 786436
  523.3 13.6 %copy-start.3 = (bf16[128,256]{1,0:T(8,128)(2,1)S(1)}, bf16[128,256]{1,0:T(8,128)(2,1)}, u32[]{:S(2)}) copy-start(bf16[128,256]{1,0:T(8,128)(2,1)} %reduce-scatter.2.cloned.1.call-done) | copy-start | bytes 196612
  524.8 15.0 %all-to-all-start.2 = ((bf16[8,16,128]{2,1,0:T(8,128)(2,1)}), bf16[8,16,128]{2,1,0:T(8,128)(2,1)S(1)}, u32[]{:S(2)}, u32[]{:S(2)}) async-start(bf16[8,16,128]{2,1,0:T(8,128)(2,1)} %bitcast.14), calls=%async_computation.3 | async-start | bytes 65536 | tf_op jit(solution)/shard_map/all_to_all | solution.py:158
  539.8 8.7 %all-to-all-start.3 = ((bf16[8,16,128]{2,1,0:T(8,128)(2,1)}), bf16[8,16,128]{2,1,0:T(8,128)(2,1)S(1)}, u32[]{:S(2)}, u32[]{:S(2)}) async-start(bf16[8,16,128]{2,1,0:T(8,128)(2,1)} %bitcast.16), calls=%async_computation.4 | async-start | bytes 65536 | tf_op jit(solution)/shard_map/all_to_all | solution.py:161
Sparse Core Ops, SparseCore 0:
  19.0 71.9 all-gather.2
  93.6 73.8 all-gather.4
  307.3 215.9 reduce-scatter.1
where the time goes:
time: 560 us; the launch traced here: 556 us
  waiting for transfers between devices  358 us (64%)
  matrix products  106 us (19%)
  other arithmetic  25.9 us (5%)
  blocking collectives  19.4 us (3%)
  local copies, waits for them, and re-layouts  14.7 us (3%)
  starting transfers between devices  14.4 us (3%)
  between operations  13.9 us (2%)
    reduce_scatter x1, waiting for transfers between devices, per_device(): lax.psum_scatter(buffer.astype(jnp.bfloat16), 'leaf', scatter_dimension=0...  216 us
    all_gather x1, waiting for transfers between devices, per_device(): value_piece = lax.all_gather(value_local, 'leaf', axis=0, tiled=True)  76.5 us
    all_gather x1, waiting for transfers between devices, per_device(): key_piece = lax.all_gather(key_local, 'leaf', axis=0, tiled=True)  59.2 us
    dot_general x32, matrix products, logits_of(): jnp.einsum('tkgd,skd->kgts', query_group, key_rows, preferred_element_typ...  37.6 us
    dot_general x16, matrix products, forward_tile(): jnp.einsum('kgts,skd->kgtd', expo.astype(jnp.bfloat16), value_rows, prefe...  21.8 us
    dot_general x16, matrix products, update_both(): jnp.einsum('kgts,skd->tkgd', dlogit, key_rows, preferred_element_type=jnp...  18.5 us
    dot_general x16, matrix products, gradient_tile(): jnp.einsum('tkgd,skd->kgts', grad_group, value_rows, preferred_element_ty...  18.1 us
    reduce_or x32, other arithmetic, visible(): jnp.any(ancestor_rows[:, :, None] == key_tag[None, None, :], axis=1)  13 us
  transfers between devices with their start and end apart: 5, of which 5 were waited for; matrix products, arithmetic and copies ran while one was open for 1% of the time, Pallas kernels for 0%

commit v1 on v0

v1 whole, which is shorter than its diff:
```python
import functools

import jax
import jax.numpy as jnp
from jax import lax
from jax.experimental import pallas as pl
from jax.experimental.pallas import tpu as pltpu
from jax.sharding import PartitionSpec as P

QH = 64
KVH = 8
HD = 128
BLK = 128
ANC = 8
NODES = 32
GROUP = QH // KVH
KEYS = ANC * BLK
PAIR = 2
CHUNK = 256
LOG2E = 1.4426950408889634
SCALE = HD ** (-0.5)
FAR = -1e30

NT = (((1,), (1,)), ((), ()))
NN = (((1,), (0,)), ((), ()))


def dot(a, b, dims=NN):
    return lax.dot_general(a, b, dims, preferred_element_type=jnp.float32)


def pick_kernel(anc_ref, rows_ref, out_ref):
    anc = anc_ref[...].reshape(NODES, 1, ANC, 128)
    head = lax.broadcasted_iota(jnp.int32, (NODES, KVH, ANC, 128), 1)
    want = (jnp.broadcast_to(anc, (NODES, KVH, ANC, 128)) * KVH + head).reshape(NODES * KVH * ANC, 128)
    lane = lax.broadcasted_iota(jnp.int32, (NODES * KVH * ANC, 128), 1)
    total = jnp.zeros((NODES * KVH * ANC, HD), jnp.float32)
    halves = []
    for part in range(2):
        halves.append(jnp.where(want == lane + part * 128, 1.0, 0.0).astype(jnp.bfloat16))
    onehot = jnp.concatenate(halves, axis=1)
    out_ref[...] = dot(onehot, rows_ref[...]).astype(jnp.bfloat16)


def add_kernel(code_ref, terms_ref, out_ref):
    row = lax.broadcasted_iota(jnp.int32, (NODES * KVH, NODES * KVH * ANC), 0)
    onehot = jnp.where(code_ref[...] == row, 1.0, 0.0).astype(jnp.bfloat16)
    out_ref[...] = dot(onehot, terms_ref[...]).astype(jnp.bfloat16)


def attention_kernel(
    leaf_ref, anc_ref, len_ref, q_ref, g_ref, kv_ref, out_ref, qg_ref, kvg_ref,
    k_ref, v_ref, kt_ref, vt_ref, e_ref, p_ref, dl_ref, qa_ref, ga_ref,
):
    step = pl.program_id(0)
    leaf = leaf_ref[0]
    wide = PAIR * BLK

    @pl.when(step == 0)
    def _():
        for rr in range(16):
            k_ref[pl.ds(rr * 64, 64), :] = kv_ref[pl.ds(rr * 128, 64), :]
            v_ref[pl.ds(rr * 64, 64), :] = kv_ref[pl.ds(rr * 128 + 64, 64), :]
        kt_ref[...] = k_ref[...].T
        vt_ref[...] = v_ref[...].T

    slot = lax.broadcasted_iota(jnp.int32, (ANC, wide), 0)
    query = lax.broadcasted_iota(jnp.int32, (ANC, wide), 1) % BLK
    limit = jnp.zeros((ANC, wide), jnp.int32)
    for s in range(ANC):
        node = anc_ref[leaf, s]
        length = jnp.where(node >= 0, len_ref[jnp.maximum(node, 0)], 0)
        own = jnp.where(node == leaf, 1, 0)
        here = jnp.where(own == 1, jnp.minimum(query + 1, length), length)
        limit = jnp.where(slot == s, here, limit)

    q2 = jnp.concatenate([q_ref[:, :HD], q_ref[:, HD:]], axis=0)
    g2 = jnp.concatenate([g_ref[:, :HD], g_ref[:, HD:]], axis=0)
    qa_ref[pl.ds(step * wide, wide), :] = q2
    ga_ref[pl.ds(step * wide, wide), :] = g2
    groups = CHUNK // ANC
    tall = jnp.broadcast_to(limit[None], (groups, ANC, wide))
    index = lax.broadcasted_iota(jnp.int32, (groups, ANC, wide), 0)

    top = jnp.full((ANC, wide), FAR, jnp.float32)
    for c in range(KEYS // CHUNK):
        raw = dot(k_ref[pl.ds(c * CHUNK, CHUNK), :], q2, NT) * (SCALE * LOG2E)
        number = index + c * groups
        place = (number % 8) * 16 + number // 8
        masked = jnp.where(place < tall, raw.reshape(groups, ANC, wide), FAR)
        top = jnp.maximum(top, jnp.max(masked, axis=0))
        e_ref[pl.ds(c * CHUNK, CHUNK), :] = masked.reshape(CHUNK, wide)
    row_top = jnp.max(top, axis=0, keepdims=True)
    part = jnp.zeros((ANC, wide), jnp.float32)
    acc = jnp.zeros((HD, wide), jnp.float32)
    for c in range(KEYS // CHUNK):
        expo = jnp.exp2(e_ref[pl.ds(c * CHUNK, CHUNK), :] - row_top)
        e_ref[pl.ds(c * CHUNK, CHUNK), :] = expo
        part = part + jnp.sum(expo.reshape(groups, ANC, wide), axis=0)
        acc = acc + dot(vt_ref[:, pl.ds(c * CHUNK, CHUNK)], expo.astype(jnp.bfloat16))
    total = jnp.sum(part, axis=0, keepdims=True)
    inverse = 1.0 / total
    out_t = (acc * inverse).astype(jnp.bfloat16)
    gt = g2.T
    delta = jnp.sum(gt.astype(jnp.float32) * out_t.astype(jnp.float32), axis=0, keepdims=True)
    for i in range(PAIR):
        out_ref[:, pl.ds(i * HD, HD)] = out_t[:, i * BLK : (i + 1) * BLK].T
    qacc = jnp.zeros((HD, wide), jnp.float32)
    for c in range(KEYS // CHUNK):
        dprob = dot(v_ref[pl.ds(c * CHUNK, CHUNK), :], g2, NT)
        weights = e_ref[pl.ds(c * CHUNK, CHUNK), :] * inverse
        dlogit = (weights * (dprob - delta)).astype(jnp.bfloat16)
        p_ref[step, pl.ds(c * CHUNK, CHUNK), :] = weights.astype(jnp.bfloat16)
        dl_ref[step, pl.ds(c * CHUNK, CHUNK), :] = dlogit
        qacc = qacc + dot(kt_ref[:, pl.ds(c * CHUNK, CHUNK)], dlogit)
    qacc = qacc * SCALE
    for i in range(PAIR):
        qg_ref[:, pl.ds(i * HD, HD)] = qacc[:, i * BLK : (i + 1) * BLK].T

    @pl.when(step == pl.num_programs(0) - 1)
    def _():
        for c in range(KEYS // CHUNK):
            kg = jnp.zeros((CHUNK, HD), jnp.float32)
            vg = jnp.zeros((CHUNK, HD), jnp.float32)
            for b in range(GROUP // PAIR):
                kg = kg + dot(dl_ref[b, pl.ds(c * CHUNK, CHUNK), :], qa_ref[pl.ds(b * wide, wide), :])
                vg = vg + dot(p_ref[b, pl.ds(c * CHUNK, CHUNK), :], ga_ref[pl.ds(b * wide, wide), :])
            kg = (kg * SCALE).astype(jnp.bfloat16)
            vg = vg.astype(jnp.bfloat16)
            for r in range(CHUNK // 64):
                rr = c * (CHUNK // 64) + r
                kvg_ref[pl.ds(rr * 128, 64), :] = kg[r * 64 : (r + 1) * 64]
                kvg_ref[pl.ds(rr * 128 + 64, 64), :] = vg[r * 64 : (r + 1) * 64]


def attend(leaf, ancestry, node_len, query, grad, kv):
    wide = PAIR * HD
    whole = lambda shape: pl.BlockSpec(shape, lambda i, *_: (0,) * len(shape))
    pair = lambda: pl.BlockSpec((BLK, wide), lambda i, *_: (0, i))
    steps = GROUP // PAIR
    return pl.pallas_call(
        attention_kernel,
        out_shape=(
            jax.ShapeDtypeStruct((BLK, GROUP * HD), jnp.bfloat16),
            jax.ShapeDtypeStruct((BLK, GROUP * HD), jnp.float32),
            jax.ShapeDtypeStruct((2 * KEYS, HD), jnp.bfloat16),
        ),
        grid_spec=pltpu.PrefetchScalarGridSpec(
            num_scalar_prefetch=3,
            grid=(steps,),
            in_specs=[pair(), pair(), whole((2 * KEYS, HD))],
            out_specs=[pair(), pair(), whole((2 * KEYS, HD))],
            scratch_shapes=[
                pltpu.VMEM((KEYS, HD), jnp.bfloat16),
                pltpu.VMEM((KEYS, HD), jnp.bfloat16),
                pltpu.VMEM((HD, KEYS), jnp.bfloat16),
                pltpu.VMEM((HD, KEYS), jnp.bfloat16),
                pltpu.VMEM((KEYS, PAIR * BLK), jnp.float32),
                pltpu.VMEM((steps, KEYS, PAIR * BLK), jnp.bfloat16),
                pltpu.VMEM((steps, KEYS, PAIR * BLK), jnp.bfloat16),
                pltpu.VMEM((GROUP * BLK, HD), jnp.bfloat16),
                pltpu.VMEM((GROUP * BLK, HD), jnp.bfloat16),
            ],
        ),
        compiler_params=pltpu.CompilerParams(dimension_semantics=("arbitrary",)),
        name="attend",
    )(leaf, ancestry, node_len, query, grad, kv)


def per_device(query_in, key_in, value_in, out_grad, ancestry, node_len):
    leaf = lax.axis_index("leaf").astype(jnp.int32).reshape(1)
    rows = key_in.shape[0]
    pieces = jnp.stack([key_in.reshape(rows, KVH, HD), value_in.reshape(rows, KVH, HD)], axis=1)
    pieces = pieces.reshape(2 * rows, KVH, HD)
    gathered = lax.all_to_all(pieces, "leaf", split_axis=0, concat_axis=0, tiled=True)
    wide_anc = jnp.broadcast_to(ancestry.reshape(NODES * ANC, 1), (NODES * ANC, 128))
    count = NODES * KVH * ANC
    picked = pl.pallas_call(
        pick_kernel,
        out_shape=jax.ShapeDtypeStruct((count, HD), jnp.bfloat16),
        name="pick",
    )(wide_anc, gathered.reshape(NODES * KVH, HD))
    kv = lax.all_to_all(picked, ("leaf", "head"), split_axis=0, concat_axis=0, tiled=True)
    attended, query_grad, terms = attend(leaf, ancestry, node_len, query_in, out_grad, kv)
    terms = lax.all_to_all(terms, ("leaf", "head"), split_axis=0, concat_axis=0, tiled=True)
    code = ancestry[:, None, :] * KVH + jnp.arange(KVH, dtype=jnp.int32)[None, :, None]
    summed = pl.pallas_call(
        add_kernel,
        out_shape=jax.ShapeDtypeStruct((NODES * KVH, HD), jnp.bfloat16),
        name="add",
    )(code.reshape(1, count), terms)
    back = lax.all_to_all(summed.reshape(NODES, KVH, HD), "leaf", split_axis=0, concat_axis=0, tiled=True)
    back = back.reshape(rows, 2, KVH * HD).astype(jnp.float32)
    return (attended, query_grad, back[:, 0], back[:, 1])


def solution(mesh):
    return jax.shard_map(
        per_device,
        mesh=mesh,
        in_specs=(
            P("leaf", "head"),
            P(("leaf", "head"), None),
            P(("leaf", "head"), None),
            P("leaf", "head"),
            P(),
            P(),
        ),
        out_specs=(
            P("leaf", "head"),
            P("leaf", "head"),
            P(("leaf", "head"), None),
            P(("leaf", "head"), None),
        ),
        check_vma=False,
    )
```

time: 560 us -> 108 us (0.19)
  waiting for transfers between devices: 358 us -> 47.6 us
  matrix products: 106 us -> 0 us
  other arithmetic: 25.9 us -> 0.02 us
  Pallas kernels: 0 us -> 13.9 us
  between operations: 13.9 us -> 0.73 us
  starting transfers between devices: 14.4 us -> 26.4 us
  local copies, waits for them, and re-layouts: 14.7 us -> 5.57 us
  blocking collectives: 19.4 us -> 13.3 us
    reduce_scatter x1 -> x0, waiting for transfers between devices: 216 us -> none  [per_device(): lax.psum_scatter(buffer.astype(jnp.bfloat16), 'leaf', scatter_dimension=0...]
    all_gather x2 -> x0, waiting for transfers between devices: 136 us -> none  [the longest x1 76.5 us: per_device(): value_piece = lax.all_gather(value_local, 'leaf', axis=0, tiled=True)]
    dot_general x112 -> x0, matrix products: 106 us -> none  [the longest x32 37.6 us: logits_of(): jnp.einsum('tkgd,skd->kgts', query_group, key_rows, preferred_element_typ...]
    all_to_all x2 -> x3, waiting for transfers between devices: 6.3 us -> 47.6 us  [the longest x1 19.9 us: per_device(): lax.all_to_all(picked, ('leaf', 'head'), split_axis=0, concat_axis=0, til...]
    pallas_call x0 -> x3, Pallas kernels: none -> 13.9 us  [the longest x1 9.64 us: attend(): pl.pallas_call(attention_kernel, out_shape=(jax.ShapeDtypeStruct((BLK, GR...]
    reduce_or x32 -> x0, other arithmetic: 13 us -> none  [visible(): jnp.any(ancestor_rows[:, :, None] == key_tag[None, None, :], axis=1)]
    all_to_all x2 -> x3, starting transfers between devices: 14.2 us -> 26.4 us  [the longest x1 12.2 us: per_device(): lax.all_to_all(pieces, 'leaf', split_axis=0, concat_axis=0, tiled=True)]
    all_to_all x2 -> x1, blocking collectives: 19.4 us -> 13.3 us  [per_device(): lax.all_to_all(summed.reshape(NODES, KVH, HD), 'leaf', split_axis=0, conc...]
  transfers between devices with their start and end apart: 5 -> 3, of which waited for: 5 -> 3; matrix products, arithmetic and copies ran while one was open for 1% -> 1% of each run, Pallas kernels for 0% -> 0%
where the time goes in v1:
time: 108 us; the launch traced here: 107 us
  waiting for transfers between devices  47.6 us (44%)
  starting transfers between devices  26.4 us (24%)
  Pallas kernels  13.9 us (13%)
  blocking collectives  13.3 us (12%)
  local copies, waits for them, and re-layouts  5.57 us (5%)
    all_to_all x1, waiting for transfers between devices, per_device(): lax.all_to_all(picked, ('leaf', 'head'), split_axis=0, concat_axis=0, til...  19.9 us
    all_to_all x1, waiting for transfers between devices, per_device(): lax.all_to_all(terms, ('leaf', 'head'), split_axis=0, concat_axis=0, tile...  19.1 us
    all_to_all x1, blocking collectives, per_device(): lax.all_to_all(summed.reshape(NODES, KVH, HD), 'leaf', split_axis=0, conc...  13.3 us
    all_to_all x1, starting transfers between devices, per_device(): lax.all_to_all(pieces, 'leaf', split_axis=0, concat_axis=0, tiled=True)  12.2 us
    pallas_call x1, Pallas kernels, attend(): pl.pallas_call(attention_kernel, out_shape=(jax.ShapeDtypeStruct((BLK, GR...  9.64 us
    all_to_all x1, waiting for transfers between devices, per_device(): lax.all_to_all(pieces, 'leaf', split_axis=0, concat_axis=0, tiled=True)  8.64 us
    all_to_all x1, starting transfers between devices, per_device(): lax.all_to_all(picked, ('leaf', 'head'), split_axis=0, concat_axis=0, til...  8.08 us
    all_to_all x1, starting transfers between devices, per_device(): lax.all_to_all(terms, ('leaf', 'head'), split_axis=0, concat_axis=0, tile...  6.2 us
  transfers between devices with their start and end apart: 3, of which 3 were waited for; matrix products, arithmetic and copies ran while one was open for 1% of the time, Pallas kernels for 0%

profile of v1, /device:TPU:1, one launch (start us, length us, event | category | flops | bytes accessed | tf_op | source)
XLA Modules:
  0.0 107.5 jit_solution(6822198942410178933)
XLA Ops:
  0.6 0.0 copy-start.4
  0.6 0.8 copy.19
  1.4 0.0 copy-done.4
  1.4 0.6 copy.14
  2.1 0.0 copy-start.5
  2.1 12.2 %all-to-all-start = ((bf16[32,8,128]{2,1,0:T(8,128)(2,1)}), bf16[32,8,128]{2,1,0:T(8,128)(2,1)S(1)}, u32[]{:S(2)}, u32[]{:S(2)}) async-start(bf16[32,8,128]{2,1,0:T(8,128)(2,1)} %bitcast.1), calls=%async_computation | async-start | bytes 131072 | tf_op jit(solution)/shard_map/all_to_all | solution.py:175
  14.3 0.0 copy-done.5
  14.3 0.1 copy.15.anc_ref
  14.3 0.0 copy-start.3
  14.3 0.1 broadcast_in_dim.4
  14.4 8.6 %all-to-all-done = bf16[32,8,128]{2,1,0:T(8,128)(2,1)S(1)} async-done(((bf16[32,8,128]{2,1,0:T(8,128)(2,1)}), bf16[32,8,128]{2,1,0:T(8,128)(2,1)S(1)}, u32[]{:S(2)}, u32[]{:S(2)}) %all-to-all-start) | async-done | bytes 65568 | tf_op jit(solution)/shard_map/all_to_all | solution.py:175
  23.1 0.0 copy-start.2
  23.1 0.8 broadcast_in_dim.10.anc_ref
  23.8 0.0 copy-done.3
  23.8 0.0 copy-done.2
  23.8 2.1 %pick.1 = bf16[2048,128]{1,0:T(8,128)(2,1)} custom-call(s32[256,128]{1,0:T(8,128)} %broadcast_in_dim.10.anc_ref, bf16[256,128]{1,0:T(8,128)(2,1)} %bitcast.25), custom_call_target="tpu_custom_call" | custom-call | tf_op jit(solution)/shard_map/pick/pallas_call | solution.py:178
  26.0 8.1 %all-to-all-start.1 = ((bf16[256,8,128]{2,1,0:T(8,128)(2,1)}), bf16[256,8,128]{2,1,0:T(8,128)(2,1)S(1)}, u32[]{:S(2)}, u32[]{:S(2)}) async-start(bf16[256,8,128]{2,1,0:T(8,128)(2,1)} %bitcast.22), calls=%async_computation.1 | async-start | bytes 1048576 | tf_op jit(solution)/shard_map/all_to_all | solution.py:183
  34.1 19.9 %all-to-all-done.1 = bf16[256,8,128]{2,1,0:T(8,128)(2,1)S(1)} async-done(((bf16[256,8,128]{2,1,0:T(8,128)(2,1)}), bf16[256,8,128]{2,1,0:T(8,128)(2,1)S(1)}, u32[]{:S(2)}, u32[]{:S(2)}) %all-to-all-start.1) | async-done | bytes 524320 | tf_op jit(solution)/shard_map/all_to_all | solution.py:183
  54.0 0.0 copy-start
  54.0 0.8 copy-done
  54.7 9.6 %attend.1 = (bf16[128,1024]{1,0:T(8,128)(2,1)}, f32[128,1024]{1,0:T(8,128)}, bf16[2048,128]{1,0:T(8,128)(2,1)}) custom-call(s32[1]{0:T(128)} %bitcast.leaf_ref, s32[32,8]{1,0:T(8,128)} %copy-done.3, s32[32]{0:T(128)} %len_ref.1, bf16[128,1024]{1,0:T(8,128)(2,1)} %q_ref.1, bf16[128,1024]{1,0:T(8,128)(2,1)} %g_ref.1, bf16[2048,128]{1,0:T(8,128)(2,1)} %bitcast.20), custom_call_target="tpu_custom_call" | custom-call | tf_op jit(solution)/shard_map/attend/pallas_call | solution.py:141
  64.4 6.2 %all-to-all-start.2 = ((bf16[256,8,128]{2,1,0:T(8,128)(2,1)}), bf16[256,8,128]{2,1,0:T(8,128)(2,1)S(1)}, u32[]{:S(2)}, u32[]{:S(2)}) async-start(bf16[256,8,128]{2,1,0:T(8,128)(2,1)} %bitcast.23), calls=%async_computation.2 | async-start | bytes 1048576 | tf_op jit(solution)/shard_map/all_to_all | solution.py:185
  70.6 0.1 copy.16
  70.7 0.7 add.27.code_ref
  71.4 19.1 %all-to-all-done.2 = bf16[256,8,128]{2,1,0:T(8,128)(2,1)S(1)} async-done(((bf16[256,8,128]{2,1,0:T(8,128)(2,1)}), bf16[256,8,128]{2,1,0:T(8,128)(2,1)S(1)}, u32[]{:S(2)}, u32[]{:S(2)}) %all-to-all-start.2) | async-done | bytes 524320 | tf_op jit(solution)/shard_map/all_to_all | solution.py:185
  90.5 0.0 copy-start.1
  90.5 0.8 copy-done.1
  91.3 2.1 %add.31 = bf16[256,128]{1,0:T(8,128)(2,1)} custom-call(s32[1,2048]{1,0:T(1,128)} %add.27.code_ref, bf16[2048,128]{1,0:T(8,128)(2,1)} %bitcast.21), custom_call_target="tpu_custom_call" | custom-call | tf_op jit(solution)/shard_map/add/pallas_call | solution.py:187
  93.4 13.3 %all_to_all.32 = bf16[32,8,128]{2,1,0:T(8,128)(2,1)S(1)} all-to-all(bf16[32,8,128]{2,1,0:T(8,128)(2,1)} %bitcast.24), channel_id=1, replica_groups=mesh['leaf'=32,'head'=8] {'leaf'}, dimensions={0} | all-to-all | bytes 131072 | tf_op jit(solution)/shard_map/all_to_all | solution.py:192
  106.6 0.1 reshape.58
  106.7 0.1 fusion
  106.8 0.7 copy_bitcast_fusion
  (4 shorter events, 0.0 us)
Async XLA Ops:
  0.6 0.8 copy-start.4
  2.1 12.2 %copy-start.5 = (s32[32,8]{0,1:T(8,128)S(1)}, s32[32,8]{0,1:T(8,128)}, u32[]{:S(2)}) copy-start(s32[32,8]{0,1:T(8,128)} %param.10) | copy-start | bytes 3076
  2.1 21.0 %all-to-all-start = ((bf16[32,8,128]{2,1,0:T(8,128)(2,1)}), bf16[32,8,128]{2,1,0:T(8,128)(2,1)S(1)}, u32[]{:S(2)}, u32[]{:S(2)}) async-start(bf16[32,8,128]{2,1,0:T(8,128)(2,1)} %bitcast.1), calls=%async_computation | async-start | bytes 131072 | tf_op jit(solution)/shard_map/all_to_all | solution.py:175
  14.3 9.5 %copy-start.3 = (s32[32,8]{1,0:T(8,128)}, s32[32,8]{1,0:T(8,128)S(1)}, u32[]{:S(2)}) copy-start(s32[32,8]{1,0:T(8,128)S(1)} %copy.15.anc_ref) | copy-start | bytes 3076
  23.1 0.8 copy-start.2
  26.0 28.0 %all-to-all-start.1 = ((bf16[256,8,128]{2,1,0:T(8,128)(2,1)}), bf16[256,8,128]{2,1,0:T(8,128)(2,1)S(1)}, u32[]{:S(2)}, u32[]{:S(2)}) async-start(bf16[256,8,128]{2,1,0:T(8,128)(2,1)} %bitcast.22), calls=%async_computation.1 | async-start | bytes 1048576 | tf_op jit(solution)/shard_map/all_to_all | solution.py:183
  54.0 0.8 copy-start
  64.4 26.1 %all-to-all-start.2 = ((bf16[256,8,128]{2,1,0:T(8,128)(2,1)}), bf16[256,8,128]{2,1,0:T(8,128)(2,1)S(1)}, u32[]{:S(2)}, u32[]{:S(2)}) async-start(bf16[256,8,128]{2,1,0:T(8,128)(2,1)} %bitcast.23), calls=%async_computation.2 | async-start | bytes 1048576 | tf_op jit(solution)/shard_map/all_to_all | solution.py:185
  90.5 0.8 copy-start.1

commit v2 on v1

v2 whole, which is shorter than its diff:
```python
import functools

import jax
import jax.numpy as jnp
from jax import lax
from jax.experimental import pallas as pl
from jax.experimental.pallas import tpu as pltpu
from jax.sharding import PartitionSpec as P

QH = 64
KVH = 8
HD = 128
BLK = 128
ANC = 8
NODES = 32
GROUP = QH // KVH
PAIR = 2
CHUNK = 128
SIZES = (4, 5, 6, 8)
LOG2E = 1.4426950408889634
SCALE = HD ** (-0.5)
FAR = -1e30

NT = (((1,), (1,)), ((), ()))
NN = (((1,), (0,)), ((), ()))


def dot(a, b, dims=NN):
    return lax.dot_general(a, b, dims, preferred_element_type=jnp.float32)


def pick_kernel(slots, anc_ref, rows_ref, out_ref):
    for l in range(NODES):
        for s in range(slots):
            node = jnp.maximum(anc_ref[l, s], 0)
            block = rows_ref[pl.ds(pl.multiple_of(node * KVH, KVH), KVH), :]
            out_ref[pl.ds((l * slots + s) * KVH, KVH), :] = block.astype(jnp.bfloat16)


def add_kernel(code_ref, terms_ref, out_ref):
    row = lax.broadcasted_iota(jnp.int32, (NODES * KVH, terms_ref.shape[0]), 0)
    onehot = jnp.where(code_ref[...] == row, 1.0, 0.0).astype(jnp.bfloat16)
    out_ref[...] = dot(onehot, terms_ref[...])


def attention_kernel(
    slots, leaf_ref, anc_ref, len_ref, q_ref, g_ref, kv_ref, out_ref, qg_ref, kvg_ref,
    k_ref, v_ref, kt_ref, vt_ref, b_ref, e_ref, p_ref, dl_ref, qa_ref, ga_ref,
):
    step = pl.program_id(0)
    leaf = leaf_ref[0]
    wide = PAIR * BLK
    keys = slots * BLK
    band = slots * KVH

    @pl.when(step == 0)
    def _():
        for rr in range(16):
            k_ref[pl.ds(rr * band, band), :] = kv_ref[pl.ds(2 * rr * band, band), :]
            v_ref[pl.ds(rr * band, band), :] = kv_ref[pl.ds((2 * rr + 1) * band, band), :]
        kt_ref[...] = k_ref[...].T
        vt_ref[...] = v_ref[...].T
        place = lax.broadcasted_iota(jnp.int32, (KVH, BLK), 0) * 16
        query = lax.broadcasted_iota(jnp.int32, (KVH, BLK), 1)
        for s in range(slots):
            node = anc_ref[leaf, s]
            length = jnp.where(node >= 0, len_ref[jnp.maximum(node, 0)], 0)
            ends = jnp.where(node == leaf, jnp.minimum(query + 1, length), length) - place
            for rr in range(16):
                b_ref[pl.ds(rr * band + s * KVH, KVH), :] = jnp.where(rr < ends, 0.0, FAR)

    q2 = jnp.concatenate([q_ref[:, :HD], q_ref[:, HD:]], axis=0)
    g2 = jnp.concatenate([g_ref[:, :HD], g_ref[:, HD:]], axis=0)
    qa_ref[pl.ds(step * wide, wide), :] = q2
    ga_ref[pl.ds(step * wide, wide), :] = g2

    top = jnp.full((KVH, wide), FAR, jnp.float32)
    for c in range(keys // CHUNK):
        rows = pl.ds(c * CHUNK, CHUNK)
        bias = b_ref[rows, :]
        raw = dot(k_ref[rows, :], q2, NT) * (SCALE * LOG2E) + jnp.concatenate([bias, bias], axis=1)
        top = jnp.maximum(top, jnp.max(raw.reshape(CHUNK // KVH, KVH, wide), axis=0))
        e_ref[rows, :] = raw
    row_top = jnp.max(top, axis=0, keepdims=True)
    part = jnp.zeros((KVH, wide), jnp.float32)
    acc = jnp.zeros((HD, wide), jnp.float32)
    for c in range(keys // CHUNK):
        rows = pl.ds(c * CHUNK, CHUNK)
        expo = jnp.exp2(e_ref[rows, :] - row_top)
        e_ref[rows, :] = expo
        part = part + jnp.sum(expo.reshape(CHUNK // KVH, KVH, wide), axis=0)
        acc = acc + dot(vt_ref[:, rows], expo.astype(jnp.bfloat16))
    total = jnp.sum(part, axis=0, keepdims=True)
    inverse = 1.0 / total
    out_t = (acc * inverse).astype(jnp.bfloat16)
    gt = g2.T
    delta = jnp.sum(gt.astype(jnp.float32) * out_t.astype(jnp.float32), axis=0, keepdims=True)
    for i in range(PAIR):
        out_ref[:, pl.ds(i * HD, HD)] = out_t[:, i * BLK : (i + 1) * BLK].T
    qacc = jnp.zeros((HD, wide), jnp.float32)
    for c in range(keys // CHUNK):
        rows = pl.ds(c * CHUNK, CHUNK)
        dprob = dot(v_ref[rows, :], g2, NT)
        weights = e_ref[rows, :] * inverse
        dlogit = (weights * (dprob - delta)).astype(jnp.bfloat16)
        p_ref[step, rows, :] = weights.astype(jnp.bfloat16)
        dl_ref[step, rows, :] = dlogit
        qacc = qacc + dot(kt_ref[:, rows], dlogit)
    qacc = qacc * SCALE
    for i in range(PAIR):
        qg_ref[:, pl.ds(i * HD, HD)] = qacc[:, i * BLK : (i + 1) * BLK].T

    @pl.when(step == pl.num_programs(0) - 1)
    def _():
        for rr in range(16):
            rows = pl.ds(rr * band, band)
            kg = jnp.zeros((band, HD), jnp.float32)
            vg = jnp.zeros((band, HD), jnp.float32)
            for b in range(GROUP // PAIR):
                kg = kg + dot(dl_ref[b, rows, :], qa_ref[pl.ds(b * wide, wide), :])
                vg = vg + dot(p_ref[b, rows, :], ga_ref[pl.ds(b * wide, wide), :])
            kvg_ref[pl.ds(2 * rr * band, band), :] = (kg * SCALE).astype(jnp.bfloat16)
            kvg_ref[pl.ds((2 * rr + 1) * band, band), :] = vg.astype(jnp.bfloat16)


def attend(slots, leaf, ancestry, node_len, query, grad, kv):
    wide = PAIR * HD
    keys = slots * BLK
    whole = lambda shape: pl.BlockSpec(shape, lambda i, *_: (0,) * len(shape))
    pair = lambda: pl.BlockSpec((BLK, wide), lambda i, *_: (0, i))
    steps = GROUP // PAIR
    return pl.pallas_call(
        functools.partial(attention_kernel, slots),
        out_shape=(
            jax.ShapeDtypeStruct((BLK, GROUP * HD), jnp.bfloat16),
            jax.ShapeDtypeStruct((BLK, GROUP * HD), jnp.float32),
            jax.ShapeDtypeStruct((2 * keys, HD), jnp.bfloat16),
        ),
        grid_spec=pltpu.PrefetchScalarGridSpec(
            num_scalar_prefetch=3,
            grid=(steps,),
            in_specs=[pair(), pair(), pl.BlockSpec(memory_space=pltpu.VMEM)],
            out_specs=[pair(), pair(), whole((2 * keys, HD))],
            scratch_shapes=[
                pltpu.VMEM((keys, HD), jnp.bfloat16),
                pltpu.VMEM((keys, HD), jnp.bfloat16),
                pltpu.VMEM((HD, keys), jnp.bfloat16),
                pltpu.VMEM((HD, keys), jnp.bfloat16),
                pltpu.VMEM((keys, BLK), jnp.float32),
                pltpu.VMEM((keys, PAIR * BLK), jnp.float32),
                pltpu.VMEM((steps, keys, PAIR * BLK), jnp.bfloat16),
                pltpu.VMEM((steps, keys, PAIR * BLK), jnp.bfloat16),
                pltpu.VMEM((GROUP * BLK, HD), jnp.bfloat16),
                pltpu.VMEM((GROUP * BLK, HD), jnp.bfloat16),
            ],
        ),
        compiler_params=pltpu.CompilerParams(dimension_semantics=("arbitrary",)),
        name=f"attend{slots}",
    )(leaf, ancestry, node_len, query, grad, kv)


def near(x):
    return pltpu.with_memory_space_constraint(x, pltpu.VMEM)


def exchange(slots, leaf, ancestry, node_len, query, grad, rows):
    count = NODES * slots * KVH
    picked = pl.pallas_call(
        functools.partial(pick_kernel, slots),
        out_shape=jax.ShapeDtypeStruct((count, HD), jnp.bfloat16),
        in_specs=[pl.BlockSpec(memory_space=pltpu.SMEM), pl.BlockSpec(memory_space=pltpu.VMEM)],
        name=f"pick{slots}",
    )(ancestry, near(rows))
    kv = lax.all_to_all(picked, "leaf", split_axis=0, concat_axis=0, tiled=True)
    attended, query_grad, terms = attend(slots, leaf, ancestry, node_len, query, grad, near(kv))
    terms = lax.all_to_all(terms, "leaf", split_axis=0, concat_axis=0, tiled=True)
    code = ancestry[:, :slots, None] * KVH + jnp.arange(KVH, dtype=jnp.int32)
    summed = pl.pallas_call(
        add_kernel,
        out_shape=jax.ShapeDtypeStruct((NODES * KVH, HD), jnp.float32),
        name=f"add{slots}",
    )(code.reshape(1, count), near(terms))
    return attended, query_grad, summed


def per_device(query_in, key_in, value_in, out_grad, ancestry, node_len):
    everyone = ("leaf", "head")
    leaf = lax.axis_index("leaf").astype(jnp.int32).reshape(1)
    rows = key_in.shape[0]
    pieces = jnp.stack([key_in.reshape(rows, KVH, HD), value_in.reshape(rows, KVH, HD)], axis=1)
    pieces = pieces.reshape(2 * rows * KVH, HD).astype(jnp.float32)
    gathered = lax.all_to_all(pieces, everyone, split_axis=0, concat_axis=0, tiled=True)
    used = jnp.max(jnp.sum((ancestry >= 0).astype(jnp.int32), axis=1))
    index = sum((used > size).astype(jnp.int32) for size in SIZES[:-1])
    branches = [functools.partial(exchange, size) for size in SIZES]
    args = (leaf, ancestry, node_len, query_in, out_grad, gathered)
    if len(SIZES) == 1:
        attended, query_grad, summed = branches[0](*args)
    else:
        attended, query_grad, summed = lax.switch(index, branches, *args)
    back = lax.all_to_all(summed, everyone, split_axis=0, concat_axis=0, tiled=True)
    back = back.reshape(rows, 2, KVH * HD)
    return (attended, query_grad, back[:, 0], back[:, 1])


def solution(mesh):
    return jax.shard_map(
        per_device,
        mesh=mesh,
        in_specs=(
            P("leaf", "head"),
            P(("leaf", "head"), None),
            P(("leaf", "head"), None),
            P("leaf", "head"),
            P(),
            P(),
        ),
        out_specs=(
            P("leaf", "head"),
            P("leaf", "head"),
            P(("leaf", "head"), None),
            P(("leaf", "head"), None),
        ),
        check_vma=False,
    )
```

time: 108 us -> 103 us (0.954); the launches traced: 107 us -> 104 us
  blocking collectives: 13.3 us -> 39.1 us
  waiting for transfers between devices: 47.6 us -> 22.3 us
  starting transfers between devices: 26.4 us -> 20.7 us
  other arithmetic: 0.02 us -> 2.38 us
  Pallas kernels: 13.9 us -> 11.8 us
  between operations: 0.73 us -> 2.68 us
  local copies, waits for them, and re-layouts: 5.57 us -> 4.2 us
    all_to_all x1 -> x2, blocking collectives: 13.3 us -> 39.1 us  [the longest x1 21.3 us: per_device(): lax.all_to_all(summed, everyone, split_axis=0, concat_axis=0, tiled=True)]
    all_to_all x3 -> x2, waiting for transfers between devices: 47.6 us -> 22.3 us  [the longest x1 12 us: exchange(): lax.all_to_all(terms, 'leaf', split_axis=0, concat_axis=0, tiled=True)]
    all_to_all x3 -> x2, starting transfers between devices: 26.4 us -> 20.7 us  [the longest x1 15.6 us: per_device(): lax.all_to_all(pieces, everyone, split_axis=0, concat_axis=0, tiled=True)]
    pallas_call x3, Pallas kernels: 13.9 us -> 11.8 us  [the longest x1 8.88 us: attend(): pl.pallas_call(functools.partial(attention_kernel, slots), out_shape=(jax...]
    unnamed x16 -> x13, local copies, waits for them, and re-layouts: 3.13 us -> 2.12 us
  transfers between devices with their start and end apart: 3 -> 2, of which waited for: 3 -> 2; matrix products, arithmetic and copies ran while one was open for 1% -> 1% of each run, Pallas kernels for 0% -> 0%
where the time goes in v2:
time: 103 us; the launch traced here: 104 us
  blocking collectives  39.1 us (38%)
  waiting for transfers between devices  22.3 us (22%)
  starting transfers between devices  20.7 us (20%)
  Pallas kernels  11.8 us (11%)
  local copies, waits for them, and re-layouts  4.2 us (4%)
  between operations  2.68 us (3%)
  other arithmetic  2.38 us (2%)
    all_to_all x1, blocking collectives, per_device(): lax.all_to_all(summed, everyone, split_axis=0, concat_axis=0, tiled=True)  21.3 us
    all_to_all x1, blocking collectives, exchange(): kv = lax.all_to_all(picked, 'leaf', split_axis=0, concat_axis=0, tiled=True)  17.8 us
    all_to_all x1, starting transfers between devices, per_device(): lax.all_to_all(pieces, everyone, split_axis=0, concat_axis=0, tiled=True)  15.6 us
    all_to_all x1, waiting for transfers between devices, exchange(): lax.all_to_all(terms, 'leaf', split_axis=0, concat_axis=0, tiled=True)  12 us
    all_to_all x1, waiting for transfers between devices, per_device(): lax.all_to_all(pieces, everyone, split_axis=0, concat_axis=0, tiled=True)  10.3 us
    pallas_call x1, Pallas kernels, attend(): pl.pallas_call(functools.partial(attention_kernel, slots), out_shape=(jax...  8.88 us
    all_to_all x1, starting transfers between devices, exchange(): lax.all_to_all(terms, 'leaf', split_axis=0, concat_axis=0, tiled=True)  5.03 us
    unnamed x13, local copies, waits for them, and re-layouts  2.12 us
  transfers between devices with their start and end apart: 2, of which 2 were waited for; matrix products, arithmetic and copies ran while one was open for 1% of the time, Pallas kernels for 0%

profile of v2, /device:TPU:1, one launch (start us, length us, event | category | flops | bytes accessed | tf_op | source)
XLA Modules:
  0.0 103.6 jit_solution(12201328784522306258)
XLA Ops:
  0.6 0.0 copy-start.7
  0.6 0.8 copy.31
  1.4 0.0 copy-done.7
  1.4 0.0 copy-start.1
  1.4 0.0 copy-start
  1.5 0.7 maximum_convert_fusion
  2.1 0.0 copy-start.6
  2.1 15.6 %all-to-all-start.8 = ((f32[256,1,128]{2,1,0:T(1,128)}), f32[256,1,128]{2,1,0:T(1,128)S(1)}, u32[]{:S(2)}, u32[]{:S(2)}) async-start(f32[256,1,128]{2,1,0:T(1,128)} %bitcast.18), calls=%async_computation.8 | async-start | bytes 262144 | tf_op jit(solution)/shard_map/all_to_all | solution.py:192
  17.8 0.0 copy-done.6
  17.8 0.6 reduce_max.9
  20.4 10.3 %all-to-all-done.8 = f32[256,1,128]{2,1,0:T(1,128)S(1)} async-done(((f32[256,1,128]{2,1,0:T(1,128)}), f32[256,1,128]{2,1,0:T(1,128)S(1)}, u32[]{:S(2)}, u32[]{:S(2)}) %all-to-all-start.8) | async-done | bytes 131104 | tf_op jit(solution)/shard_map/all_to_all | solution.py:192
  30.7 0.0 copy-start.8
  30.7 0.0 copy-done.1
  30.7 0.0 copy-done
  30.7 0.6 copy-done.8
  31.4 48.6 %conditional.1 = (bf16[128,1024]{1,0:T(8,128)(2,1)}, f32[128,1024]{1,0:T(8,128)}, f32[256,128]{1,0:T(8,128)S(1)}) conditional(s32[]{:T(128)} %clamp.3, (s32[32,8]{0,1:T(8,128)S(1)}, f32[256,128]{1,0:T(8,128)S(1)}, s32[1]{0:T(128)}, s32[32]{0:T(128)S(1)}, bf16[128,1024]{1,0:T(8,128)(2,1)S(1)}, ...), branch_computations={%region_2.0_spmd, %region_3.0_spmd, %region_4.0_spmd, %region_5.0_... | conditional | flops 2304 | bytes 2655316 | solution.py:200
  31.4 0.7 copy.26.anc_ref
  32.1 1.9 %pick6.1 = bf16[1536,128]{1,0:T(8,128)(2,1)} custom-call(s32[32,8]{1,0:T(8,128)} %copy.26.anc_ref, f32[256,128]{1,0:T(8,128)S(1)} %get-tuple-element.71.rows_ref), custom_call_target="tpu_custom_call" | custom-call | tf_op jit(solution)/shard_map/cond/branch_2_fun/pick6/pallas_call | solution.py:168
  34.0 17.8 %all_to_all.84 = bf16[32,48,128]{2,1,0:T(8,128)(2,1)S(1)} all-to-all(bf16[32,48,128]{2,1,0:T(8,128)(2,1)} %bitcast.49), channel_id=1, replica_groups=mesh['leaf'=32,'head'=8] {'leaf'}, dimensions={0} | all-to-all | bytes 786432 | tf_op jit(solution)/shard_map/cond/branch_2_fun/all_to_all | solution.py:174
  51.7 8.9 %attend6.1 = (bf16[128,1024]{1,0:T(8,128)(2,1)}, f32[128,1024]{1,0:T(8,128)}, bf16[1536,128]{1,0:T(8,128)(2,1)}) custom-call(s32[1]{0:T(128)} %get-tuple-element.66.leaf_ref, s32[32,8]{1,0:T(8,128)} %copy.26.anc_ref, s32[32]{0:T(128)S(1)} %get-tuple-element.68.len_ref, bf16[128,1024]{1,0:T(8,128)(2,1)S(1)} %get-tuple-element.69.q_ref, ...), custom_call_target="tpu_custom_call" | custom-call | tf_op jit(solution)/shard_map/cond/branch_2_fun/attend6/pallas_call | solution.py:132
  60.6 0.0 copy-start.2
  60.6 5.0 %all-to-all-start.5 = ((bf16[32,48,128]{2,1,0:T(8,128)(2,1)}), bf16[32,48,128]{2,1,0:T(8,128)(2,1)S(1)}, u32[]{:S(2)}, u32[]{:S(2)}) async-start(bf16[32,48,128]{2,1,0:T(8,128)(2,1)} %bitcast.54), calls=%async_computation.5 | async-start | bytes 786432 | tf_op jit(solution)/shard_map/cond/branch_2_fun/all_to_all | solution.py:176
  65.7 0.0 copy-done.2
  65.7 0.1 iota_add_fusion.2
  65.8 0.7 add.91.code_ref
  66.5 12.0 %all-to-all-done.5 = bf16[32,48,128]{2,1,0:T(8,128)(2,1)S(1)} async-done(((bf16[32,48,128]{2,1,0:T(8,128)(2,1)}), bf16[32,48,128]{2,1,0:T(8,128)(2,1)S(1)}, u32[]{:S(2)}, u32[]{:S(2)}) %all-to-all-start.5) | async-done | bytes 393248 | tf_op jit(solution)/shard_map/cond/branch_2_fun/all_to_all | solution.py:176
  78.4 1.0 %add6.1 = f32[256,128]{1,0:T(8,128)S(1)} custom-call(s32[1,1536]{1,0:T(1,128)} %add.91.code_ref, bf16[1536,128]{1,0:T(8,128)(2,1)S(1)} %bitcast.42), custom_call_target="tpu_custom_call" | custom-call | tf_op jit(solution)/shard_map/cond/branch_2_fun/add6/pallas_call | solution.py:178
  80.0 21.3 %all_to_all.86 = f32[256,1,128]{2,1,0:T(1,128)S(1)} all-to-all(f32[256,1,128]{2,1,0:T(1,128)S(1)} %bitcast.52), channel_id=1, replica_groups=mesh['leaf'=32,'head'=8] {'leaf','head'}, dimensions={0} | all-to-all | bytes 262144 | tf_op jit(solution)/shard_map/all_to_all | solution.py:201
  101.3 0.5 broadcast.43
  101.8 0.9 reduce.3
  102.8 0.1 reshape.149
  102.8 0.1 fusion
  103.0 0.7 copy_bitcast_fusion
  (3 shorter events, 0.0 us)
Async XLA Ops:
  0.6 0.8 copy-start.7
  1.4 29.3 %copy-start.1 = (bf16[128,1024]{1,0:T(8,128)(2,1)S(1)}, bf16[128,1024]{1,0:T(8,128)(2,1)}, u32[]{:S(2)}) copy-start(bf16[128,1024]{1,0:T(8,128)(2,1)} %param.13) | copy-start | bytes 786436
  1.4 29.3 %copy-start = (bf16[128,1024]{1,0:T(8,128)(2,1)S(1)}, bf16[128,1024]{1,0:T(8,128)(2,1)}, u32[]{:S(2)}) copy-start(bf16[128,1024]{1,0:T(8,128)(2,1)} %param.10) | copy-start | bytes 786436
  2.1 15.7 %copy-start.6 = (s32[32,8]{0,1:T(8,128)S(1)}, s32[32,8]{0,1:T(8,128)}, u32[]{:S(2)}) copy-start(s32[32,8]{0,1:T(8,128)} %param.14) | copy-start | bytes 3076
  2.1 28.6 %all-to-all-start.8 = ((f32[256,1,128]{2,1,0:T(1,128)}), f32[256,1,128]{2,1,0:T(1,128)S(1)}, u32[]{:S(2)}, u32[]{:S(2)}) async-start(f32[256,1,128]{2,1,0:T(1,128)} %bitcast.18), calls=%async_computation.8 | async-start | bytes 262144 | tf_op jit(solution)/shard_map/all_to_all | solution.py:192
  30.7 0.7 copy-start.8
  60.6 5.0 %copy-start.2 = (s32[32,8]{1,0:T(8,128)S(1)}, s32[32,8]{1,0:T(8,128)}, u32[]{:S(2)}) copy-start(s32[32,8]{1,0:T(8,128)} %copy.26.anc_ref) | copy-start | bytes 3076 | tf_op jit(solution)/shard_map/cond
  60.6 17.8 %all-to-all-start.5 = ((bf16[32,48,128]{2,1,0:T(8,128)(2,1)}), bf16[32,48,128]{2,1,0:T(8,128)(2,1)S(1)}, u32[]{:S(2)}, u32[]{:S(2)}) async-start(bf16[32,48,128]{2,1,0:T(8,128)(2,1)} %bitcast.54), calls=%async_computation.5 | async-start | bytes 786432 | tf_op jit(solution)/shard_map/cond/branch_2_fun/all_to_all | solution.py:176
